TPU v7x, 32 devices: a whole 2x2x4 slice. The times are simulated.
32 devices in a mesh: groups: 2 (over y), date: 8 (over z, x), strip: 2 (over core).
Axes of the slice: x: 2, y: 2, z: 4, core: 2. Of those that a mesh axis runs over, the one named last changes fastest.
Arguments:
- slc_tiles: float32 [2, 16, 32, 1024], P(None, ('groups', 'date'), None, 'strip'), parts along dimension 1, may hold values from -6 to 6
- coreg_shift: int32 [16, 2], P(('groups', 'date')), parts along dimension 0, may hold values from -16 to 16, as said below
- center_freq: float32 [16], P('groups'), parts along dimension 0, may hold values from -0.2 to 0.2
- filter_taps: float32 [17], replicated, may hold values from 0.05 to 0.4
- owner_table: int32 [16], P('groups'), parts along dimension 0, may hold values from 0 to 7, each once
Outputs:
- phases: float32 [2, 16, 8192], P(None, 'groups', ('date', 'strip')), parts along dimension 1
There are 2 independent parts, one for each index of `groups`. A program takes and returns all parts, laid end to end along the dimension named above; an argument that names none is the same for every part. Nothing has to cross between parts.
Inputs may be any that keep to these rules, and one draw needn't show every extreme that they name: `coreg_shift`: both 16 and -16 occur in every draw. `owner_table`: a permutation: every index of date owns exactly one block.
All inputs are finite; a program needn't handle non-finite values.
Results may differ from a plain program's by a relative error of at most 0.0003.
Values sent between devices are 32-bit elements; how exact they have to be, the bound alone decides.
No kernel may reach another device: no remote copies, remote signals or barrier semaphores. Data moves between devices by JAX's collectives and lax.ppermute only.
A program may use at most 64 MiB of HBM per device.

v0:
```python
import math
import jax
import jax.numpy as jnp
from jax import lax
from jax.sharding import PartitionSpec as P

SMAX = 16
TAPS = 17
ROUNDS = 3
MINI = 8
ITERS = 3


def swapped(value, axis, bit):
    mask = 2**bit
    pairs = [(source, source ^ mask) for source in range(lax.axis_size(axis))]
    return lax.ppermute(value, axis, pairs)


def padded_2(value, sides, width):
    for axis, dim in sides:
        peers, length = (lax.axis_size(axis), value.shape[dim])
        up = [(i, (i + 1) % peers) for i in range(peers - 1)]
        down = [(j, i) for i, j in up]
        last = lax.slice_in_dim(value, length - width, length, axis=dim)
        leading = lax.slice_in_dim(value, 0, width, axis=dim)
        before = lax.ppermute(last, axis, up)
        after = lax.ppermute(leading, axis, down)
        value = jnp.concatenate([before, value, after], axis=dim)
    return value


def look_mean(field):
    layout = field.shape
    folded = field.reshape(layout[:-2] + (layout[-2] // 2, 2, layout[-1] // 2, 2))
    return jnp.sum(folded, axis=(-3, -1)) * 0.25


def partner_view(field, stride):
    layout = field.shape
    folded = field.reshape((layout[0] // (2 * stride), 2, stride) + layout[1:])
    return jnp.flip(folded, axis=1).reshape(layout)


def pair_terms(lower_re, lower_im, stride):
    layout = lower_re.shape
    folded_re = lower_re.reshape((layout[0] // stride, stride) + layout[1:])
    folded_im = lower_im.reshape((layout[0] // stride, stride) + layout[1:])
    full_shape = (2 * layout[0],) + layout[1:]
    terms_re = jnp.stack([folded_re, folded_re], axis=1).reshape(full_shape)
    terms_im = jnp.stack([folded_im, -folded_im], axis=1).reshape(full_shape)
    return (terms_re, terms_im)


def link_phase(intensity, pair_list):
    vec_re = jnp.ones_like(intensity)
    vec_im = jnp.zeros_like(intensity)
    layout = intensity.shape
    for sweep_step in range(ITERS):
        next_re = intensity * vec_re
        next_im = intensity * vec_im
        for terms_re, terms_im, stride in pair_list:
            other_re = partner_view(vec_re, stride)
            other_im = partner_view(vec_im, stride)
            next_re = next_re + terms_re * other_re - terms_im * other_im
            next_im = next_im + terms_re * other_im + terms_im * other_re
        energy = (next_re * next_re + next_im * next_im).reshape(
            (layout[0] // MINI, MINI) + layout[1:]
        )
        length = jnp.sqrt(jnp.sum(energy, axis=1, keepdims=True))
        factor = jnp.broadcast_to(1.0 / jnp.maximum(length, 1.0), energy.shape).reshape(layout)
        vec_re = next_re * factor
        vec_im = next_im * factor
    return (vec_re, vec_im)


def link_block(received):
    date_count = received.shape[1]
    item_count = received.shape[2]
    pair_list = []
    for round_bit in range(ROUNDS):
        stride = 1 << round_bit
        fields = received[2 * round_bit : 2 * round_bit + 2].reshape(
            2, date_count // (2 * stride), 2, stride, item_count
        )
        lower_ifg = jnp.moveaxis(fields, 2, 3).reshape(2, date_count // 2, 2, item_count)
        terms_re, terms_im = pair_terms(lower_ifg[0], lower_ifg[1], stride)
        pair_list.append((terms_re, terms_im, stride))
    brightness = jnp.moveaxis(received[2 * ROUNDS : 2 * ROUNDS + 2], 0, 1)
    vec_re, vec_im = link_phase(brightness, pair_list)
    return jnp.stack([vec_re, vec_im])


def band_matrix(filter_taps, rotation, block_len):
    tap_count = filter_taps.shape[0]
    offsets = jnp.arange(tap_count, dtype=jnp.float32) - tap_count // 2
    tap_re = filter_taps * jnp.cos(rotation * offsets)
    tap_im = filter_taps * jnp.sin(rotation * offsets)
    lag_grid = (
        jnp.arange(block_len + tap_count - 1, dtype=jnp.int32)[:, None]
        - jnp.arange(block_len, dtype=jnp.int32)[None, :]
    )
    picked = lag_grid[:, :, None] == jnp.arange(tap_count, dtype=jnp.int32)[None, None, :]
    mat_re = jnp.sum(jnp.where(picked, tap_re, 0.0), axis=-1)
    mat_im = jnp.sum(jnp.where(picked, tap_im, 0.0), axis=-1)
    upper_half = jnp.concatenate([mat_re, mat_im], axis=1)
    lower_half = jnp.concatenate([-mat_im, mat_re], axis=1)
    return jnp.concatenate([upper_half, lower_half], axis=0)


def band_filter(extended, matrix, block_len, tap_reach):
    components, row_count, total_cols = extended.shape
    out_cols = total_cols - 2 * tap_reach
    nblocks = out_cols // block_len
    left_rim = extended[:, :, :out_cols].reshape(components, row_count, nblocks, block_len)[
        ..., :tap_reach
    ]
    middle = extended[:, :, tap_reach : tap_reach + out_cols].reshape(
        components, row_count, nblocks, block_len
    )
    right_rim = extended[:, :, 2 * tap_reach :].reshape(components, row_count, nblocks, block_len)[
        ..., block_len - tap_reach :
    ]
    windows = jnp.concatenate([left_rim, middle, right_rim], axis=-1)
    joined = jnp.concatenate([windows[0], windows[1]], axis=-1).reshape(row_count * nblocks, -1)
    product = jnp.dot(
        joined, matrix, precision=lax.Precision.HIGHEST, preferred_element_type=jnp.float32
    )
    product = product.reshape(row_count, nblocks, 2, block_len)
    return (
        product[:, :, 0].reshape(row_count, out_cols),
        product[:, :, 1].reshape(row_count, out_cols),
    )


def trade(payload, round_bit):
    return swapped(payload, "date", round_bit)


def shards(slc_tiles, coreg_shift, center_freq, filter_taps, owner_table):
    tap_reach = TAPS // 2
    margin = SMAX + tap_reach
    own_tile = slc_tiles[:, 0]
    row_count = own_tile.shape[1]
    strip_cols = own_tile.shape[2]
    block_len = math.gcd(strip_cols, 128)
    date_count = lax.axis_size("date")
    position = lax.axis_index("date")
    padded = padded_2(own_tile, (("strip", 2),), margin)
    line_blocks = coreg_shift.shape[1]
    grouped = padded.reshape(2, line_blocks, row_count // line_blocks, padded.shape[2])

    def shift_block(segment, amount):
        return lax.dynamic_slice_in_dim(segment, SMAX + amount, strip_cols + 2 * tap_reach, axis=2)

    resampled = jax.vmap(shift_block, in_axes=(1, 0), out_axes=1)(grouped, coreg_shift[0])
    resampled = resampled.reshape(2, row_count, strip_cols + 2 * tap_reach)
    centre = resampled[:, :, tap_reach : tap_reach + strip_cols]
    brightness = look_mean(centre[0] * centre[0] + centre[1] * centre[1])
    half_rows = row_count // 2
    pixel_count = half_rows // 2 * (strip_cols // 2)
    block_pixels = pixel_count // date_count
    bright_fields = brightness.reshape(2, date_count, block_pixels)
    date_ids = jnp.arange(date_count, dtype=jnp.int32)
    own_freq = jnp.sum(jnp.where(date_ids == position, center_freq, 0.0))
    inverse = jnp.zeros((date_count,), jnp.int32).at[owner_table].set(date_ids)
    ifg_fields = []
    for round_bit in range(ROUNDS):
        stride = 1 << round_bit
        parity = position // stride % 2
        partner = jnp.bitwise_xor(position, stride)
        partner_freq = jnp.sum(jnp.where(date_ids == partner, center_freq, 0.0))
        rotation = jnp.pi * (partner_freq - own_freq)
        whole_re, whole_im = band_filter(
            resampled, band_matrix(filter_taps, rotation, block_len), block_len, tap_reach
        )
        filtered = jnp.stack([whole_re, whole_im])
        outgoing = lax.dynamic_slice_in_dim(filtered, (1 - parity) * half_rows, half_rows, axis=1)
        kept_half = lax.dynamic_slice_in_dim(filtered, parity * half_rows, half_rows, axis=1)
        arrived = trade(outgoing, round_bit)
        mine_re, mine_im = (kept_half[0], kept_half[1])
        theirs_re, theirs_im = (arrived[0], arrived[1])
        is_lower = parity == 0
        first_re = jnp.where(is_lower, mine_re, theirs_re)
        first_im = jnp.where(is_lower, mine_im, theirs_im)
        second_re = jnp.where(is_lower, theirs_re, mine_re)
        second_im = jnp.where(is_lower, theirs_im, mine_im)
        ifg_re = look_mean(first_re * second_re + first_im * second_im)
        ifg_im = look_mean(first_im * second_re - first_re * second_im)
        round_fields = jnp.stack([ifg_re, ifg_im]).reshape(2, date_count, block_pixels)
        ifg_fields.append(round_fields)
    outgoing_all = jnp.take(jnp.concatenate(ifg_fields + [bright_fields], axis=0), inverse, axis=1)
    linked = link_block(
        lax.all_to_all(outgoing_all, "date", split_axis=1, concat_axis=1, tiled=True)
    )
    return linked.reshape(2, date_count, 2 * block_pixels)


def solution(mesh):
    in_specs = (
        P(None, ("groups", "date"), None, "strip"),
        P(("groups", "date"), None),
        P("groups"),
        P(),
        P("groups"),
    )
    out_specs = P(None, "groups", ("date", "strip"))
    return jax.shard_map(shards, mesh=mesh, in_specs=in_specs, out_specs=out_specs, check_vma=False)
```

profile of v0, /device:TPU:0, one launch (start us, length us, event | category | flops | bytes accessed | tf_op | source)
XLA Modules:
  0.0 62.4 jit_solution(8768502680218335158)
XLA Ops:
  0.0 0.9 %fusion.65 = (f32[2,32,24]{2,1,0:T(8,128)S(1)}, f32[2,32,24]{2,1,0:T(8,128)S(1)}) fusion(f32[2,32,512]{2,1,0:T(8,128)} %bitcast.407), kind=kLoop, calls=%fused_computation.199 | loop fusion | bytes 24576 | tf_op jit(solution)/shard_map/slice | solution.py:25
  0.9 2.4 %collective-permute-start = (f32[2,32,24]{2,1,0:T(8,128)S(1)}, f32[2,32,24]{2,1,0:T(8,128)S(1)}, u32[]{:S(2)}, u32[]{:S(2)}) collective-permute-start(f32[2,32,24]{2,1,0:T(8,128)S(1)} %get-tuple-element.47), channel_id=1, source_target_pairs={{0,1},{2,3},{4,5},{6,7},{8,9},{10,11},{12,13},{14,15},{16,17},{18,... | collective-permute-start | bytes 18440 | tf_op jit(solution)/shard_map/ppermute | solution.py:27
  3.3 1.3 %collective-permute-start.1 = (f32[2,32,24]{2,1,0:T(8,128)S(1)}, f32[2,32,24]{2,1,0:T(8,128)S(1)}, u32[]{:S(2)}, u32[]{:S(2)}) collective-permute-start(f32[2,32,24]{2,1,0:T(8,128)S(1)} %get-tuple-element.48), channel_id=1, source_target_pairs={{1,0},{3,2},{5,4},{7,6},{9,8},{11,10},{13,12},{15,14},{17,16},{19,... | collective-permute-start | bytes 18440 | tf_op jit(solution)/shard_map/ppermute | solution.py:28
  4.6 0.7 %compare_select_fusion.2 = s32[8]{0:T(128)S(1)} fusion(s32[8]{0:T(128)} %param.9), kind=kLoop, calls=%fused_computation.163 | loop fusion | flops 24 | bytes 64 | tf_op jit(solution)/shard_map/select_n | solution.py:166
  5.3 0.6 scatter_custom_fusion
  5.9 1.3 %fusion.45 = (f32[]{:T(128)}, f32[]{:T(128)}, f32[]{:T(128)}, f32[]{:T(128)}) fusion(f32[8]{0:T(128)} %param.7, s32[]{:T(128)S(6)} %xor.11, s32[]{:T(128)S(6)} %axis_index.15, s32[]{:T(128)S(6)} %xor.9, s32[]{:T(128)S(6)} %xor.10), kind=kLoop, calls=%fused_computation.175 | loop fusion | flops 92 | bytes 64 | tf_op jit(solution)/shard_map/reduce_sum | solution.py:172
  11.2 0.7 %or_bitcast_fusion = s32[2]{0:T(128)S(1)} fusion(s32[1,2]{1,0:T(1,128)} %param.6), kind=kLoop, calls=%fused_computation.177 | loop fusion | flops 18 | bytes 16 | tf_op jit(solution)/shard_map/vmap()/gather | solution.py:154
  11.9 0.7 %cosine_multiply_fusion.2 = (f32[17]{0:T(128)S(1)}, f32[17]{0:T(128)S(1)}, f32[17]{0:T(128)S(1)}, f32[17]{0:T(128)S(1)}, f32[17]{0:T(128)S(1)}, /*index=5*/f32[17]{0:T(128)S(1)}) fusion(f32[17]{0:T(128)} %param.8, f32[]{:T(128)S(6)} %mul.430, f32[]{:T(128)S(6)} %mul.445, f32[]{:T(128)S(6)} %mul.460), kind=kLoop, calls=%fused_computation.183 | loop fusion | flops 170 | bytes 488 | tf_op jit(solution)/shard_map/mul | solution.py:97
  12.6 1.0 %select_reduce_fusion = (f32[144,128]{1,0:T(8,128)S(1)}, f32[144,128]{1,0:T(8,128)S(1)}, f32[144,128]{1,0:T(8,128)S(1)}, f32[144,128]{1,0:T(8,128)S(1)}, f32[144,128]{1,0:T(8,128)S(1)}, /*index=5*/f32[144,128]{1,0:T(8,128)S(1)}) fusion(f32[17]{0:T(128)S(1)} %get-tuple-element.68, s32[144,128]{1,0:T(8,128)S(1)} %iota_subtract_fusion, ...), kind=kLoop, calls=%fused_computation.3 | loop fusion | flops 3962880 | bytes 516504 | tf_op jit(solution)/shard_map/reduce_sum | solution.py:105
  14.0 0.8 %copy.94 = f32[2,2,16,560]{2,0,1,3:T(2,128)S(1)} copy(f32[2,2,16,560]{3,2,1,0:T(8,128)S(1)} %pad_maximum_fusion.1) | data formatting | bytes 286720 | tf_op jit(solution)/shard_map/concatenate | solution.py:29
  14.8 2.0 %gather_fusion.1 = f32[2,2,16,528]{2,1,3,0:T(2,128)S(1)} fusion(f32[2,2,16,560]{2,1,0,3:T(2,128)S(1)} %bitcast.403, s32[2]{0:T(128)S(1)} %or_bitcast_fusion), kind=kCustom, calls=%fused_computation.1 | custom fusion | bytes 270368 | tf_op jit(solution)/shard_map/vmap()/gather | solution.py:154
  16.8 0.5 copy.95
  18.1 0.4 fusion
  18.8 3.5 %collective-permute-start.4 = (f32[2,16,512]{2,0,1:T(2,128)S(1)}, f32[2,16,512]{2,0,1:T(2,128)S(1)}, u32[]{:S(2)}, u32[]{:S(2)}) collective-permute-start(f32[2,16,512]{2,0,1:T(2,128)S(1)} %get-tuple-element.36), channel_id=1, source_target_pairs={{0,8},{2,10},{4,12},{6,14},{8,0},{10,2},{12,4},{14,6},{1,9},{3,11}... | collective-permute-start | bytes 196616 | tf_op jit(solution)/shard_map/ppermute | solution.py:17
  22.2 0.4 fusion.2
  22.9 1.6 %collective-permute-start.3 = (f32[2,16,512]{2,0,1:T(2,128)S(1)}, f32[2,16,512]{2,0,1:T(2,128)S(1)}, u32[]{:S(2)}, u32[]{:S(2)}) collective-permute-start(f32[2,16,512]{2,0,1:T(2,128)S(1)} %get-tuple-element.40), channel_id=1, source_target_pairs={{0,4},{2,6},{4,0},{6,2},{8,12},{10,14},{12,8},{14,10},{1,5},{3,7},... | collective-permute-start | bytes 196616 | tf_op jit(solution)/shard_map/ppermute | solution.py:17
  24.6 0.4 fusion.4
  25.2 1.6 %collective-permute-start.2 = (f32[2,16,512]{2,0,1:T(2,128)S(1)}, f32[2,16,512]{2,0,1:T(2,128)S(1)}, u32[]{:S(2)}, u32[]{:S(2)}) collective-permute-start(f32[2,16,512]{2,0,1:T(2,128)S(1)} %get-tuple-element.44), channel_id=1, source_target_pairs={{0,2},{2,0},{4,6},{6,4},{8,10},{10,8},{12,14},{14,12},{1,3},{3,1},... | collective-permute-start | bytes 196616 | tf_op jit(solution)/shard_map/ppermute | solution.py:17
  26.8 5.5 %add.228 = f32[16,2,256,2]{3,2,1,0:T(8,128)} reshape(f32[1,32,512]{2,1,0:T(8,128)S(1)} %fusion.12) | data formatting | bytes 131072 | tf_op jit(solution)/shard_map/add | solution.py:159
  32.3 2.8 %reduce_sum.196 = f32[16,256]{1,0:T(8,128)S(1)} reduce(f32[16,2,256,2]{3,2,1,0:T(8,128)} %add.228, f32[]{:T(128)} %constant.95.clone.1), dimensions={1,3}, to_apply=%region_17.18 | reduce | flops 12288 | bytes 81924 | tf_op jit(solution)/shard_map/reduce_sum | solution.py:36
  35.4 2.1 %add.226 = f32[8,2,256,2]{3,2,1,0:T(8,128)S(1)} reshape(f32[16,512]{1,0:T(8,128)S(1)} %get-tuple-element.6) | data formatting | bytes 65536 | tf_op jit(solution)/shard_map/add | solution.py:188
  37.5 0.3 reduce_sum.194
  37.8 2.1 %sub.173 = f32[8,2,256,2]{3,2,1,0:T(8,128)S(1)} reshape(f32[16,512]{1,0:T(8,128)S(1)} %get-tuple-element.5) | data formatting | bytes 65536 | tf_op jit(solution)/shard_map/sub | solution.py:189
  39.9 0.3 reduce_sum.195
  40.6 2.1 %add.221 = f32[8,2,256,2]{3,2,1,0:T(8,128)S(1)} reshape(f32[16,512]{1,0:T(8,128)S(1)} %get-tuple-element.8) | data formatting | bytes 65536 | tf_op jit(solution)/shard_map/add | solution.py:188
  42.7 0.3 reduce_sum.189
  43.0 2.1 %sub.168 = f32[8,2,256,2]{3,2,1,0:T(8,128)S(1)} reshape(f32[16,512]{1,0:T(8,128)S(1)} %get-tuple-element.7) | data formatting | bytes 65536 | tf_op jit(solution)/shard_map/sub | solution.py:189
  45.8 2.1 %add.216 = f32[8,2,256,2]{3,2,1,0:T(8,128)S(1)} reshape(f32[16,512]{1,0:T(8,128)S(1)} %get-tuple-element.10) | data formatting | bytes 65536 | tf_op jit(solution)/shard_map/add | solution.py:188
  48.3 2.1 %sub.163 = f32[8,2,256,2]{3,2,1,0:T(8,128)S(1)} reshape(f32[16,512]{1,0:T(8,128)S(1)} %get-tuple-element.9) | data formatting | bytes 65536 | tf_op jit(solution)/shard_map/sub | solution.py:189
  50.9 0.6 gather_fusion
  51.5 9.3 %all_to_all.5 = f32[8,8,256]{2,0,1:T(8,128)S(1)} all-to-all(f32[8,8,256]{2,0,1:T(8,128)S(1)} %select_bitcast_fusion), channel_id=1, replica_groups=mesh['groups'=2,'date'=8,'strip'=2] {'date'}, dimensions={1} | all-to-all | bytes 131072 | tf_op jit(solution)/shard_map/all_to_all | solution.py:194
  61.8 0.6 pad_maximum_fusion.2
  (107 shorter events, 4.4 us)
Async XLA Ops:
  0.0 13.9 %copy-start = (f32[2,1,32,512]{3,2,1,0:T(8,128)S(1)}, f32[2,1,32,512]{3,2,1,0:T(8,128)}, u32[]{:S(2)}) copy-start(f32[2,1,32,512]{3,2,1,0:T(8,128)} %param.5) | copy-start | bytes 393220
  0.9 13.0 %collective-permute-start = (f32[2,32,24]{2,1,0:T(8,128)S(1)}, f32[2,32,24]{2,1,0:T(8,128)S(1)}, u32[]{:S(2)}, u32[]{:S(2)}) collective-permute-start(f32[2,32,24]{2,1,0:T(8,128)S(1)} %get-tuple-element.47), channel_id=1, source_target_pairs={{0,1},{2,3},{4,5},{6,7},{8,9},{10,11},{12,13},{14,15},{16,17},{18,... | collective-permute-start | bytes 18440 | tf_op jit(solution)/shard_map/ppermute | solution.py:27
  3.3 10.6 %collective-permute-start.1 = (f32[2,32,24]{2,1,0:T(8,128)S(1)}, f32[2,32,24]{2,1,0:T(8,128)S(1)}, u32[]{:S(2)}, u32[]{:S(2)}) collective-permute-start(f32[2,32,24]{2,1,0:T(8,128)S(1)} %get-tuple-element.48), channel_id=1, source_target_pairs={{1,0},{3,2},{5,4},{7,6},{9,8},{11,10},{13,12},{15,14},{17,16},{19,... | collective-permute-start | bytes 18440 | tf_op jit(solution)/shard_map/ppermute | solution.py:28
  18.8 16.4 %collective-permute-start.4 = (f32[2,16,512]{2,0,1:T(2,128)S(1)}, f32[2,16,512]{2,0,1:T(2,128)S(1)}, u32[]{:S(2)}, u32[]{:S(2)}) collective-permute-start(f32[2,16,512]{2,0,1:T(2,128)S(1)} %get-tuple-element.36), channel_id=1, source_target_pairs={{0,8},{2,10},{4,12},{6,14},{8,0},{10,2},{12,4},{14,6},{1,9},{3,11}... | collective-permute-start | bytes 196616 | tf_op jit(solution)/shard_map/ppermute | solution.py:17
  22.9 17.4 %collective-permute-start.3 = (f32[2,16,512]{2,0,1:T(2,128)S(1)}, f32[2,16,512]{2,0,1:T(2,128)S(1)}, u32[]{:S(2)}, u32[]{:S(2)}) collective-permute-start(f32[2,16,512]{2,0,1:T(2,128)S(1)} %get-tuple-element.40), channel_id=1, source_target_pairs={{0,4},{2,6},{4,0},{6,2},{8,12},{10,14},{12,8},{14,10},{1,5},{3,7},... | collective-permute-start | bytes 196616 | tf_op jit(solution)/shard_map/ppermute | solution.py:17
  25.2 20.3 %collective-permute-start.2 = (f32[2,16,512]{2,0,1:T(2,128)S(1)}, f32[2,16,512]{2,0,1:T(2,128)S(1)}, u32[]{:S(2)}, u32[]{:S(2)}) collective-permute-start(f32[2,16,512]{2,0,1:T(2,128)S(1)} %get-tuple-element.44), channel_id=1, source_target_pairs={{0,2},{2,0},{4,6},{6,4},{8,10},{10,8},{12,14},{14,12},{1,3},{3,1},... | collective-permute-start | bytes 196616 | tf_op jit(solution)/shard_map/ppermute | solution.py:17
where the time goes:
time: 62.7 us; the launch traced here: 62.4 us
  local copies, waits for them, and re-layouts  24.4 us (39%)
  other arithmetic  12.2 us (19%)
  starting transfers between devices  10.4 us (17%)
  blocking collectives  9.28 us (15%)
  between operations  4.92 us (8%)
  matrix products  1.25 us (2%)
    all_to_all x1, blocking collectives, shards(): lax.all_to_all(outgoing_all, 'date', split_axis=1, concat_axis=1, tiled=T...  9.28 us
    ppermute x3, starting transfers between devices, swapped(): return lax.ppermute(value, axis, pairs)  6.67 us
    sub x3, local copies, waits for them, and re-layouts, shards(): ifg_im = look_mean(first_im * second_re - first_re * second_im)  6.25 us
    add x3, local copies, waits for them, and re-layouts, shards(): ifg_re = look_mean(first_re * second_re + first_im * second_im)  6.25 us
    add x1, local copies, waits for them, and re-layouts, shards(): brightness = look_mean(centre[0] * centre[0] + centre[1] * centre[1])  5.48 us
    reduce_sum x7, other arithmetic, look_mean(): return jnp.sum(folded, axis=(-3, -1)) * 0.25  4.88 us
    ppermute x1, starting transfers between devices, padded_2(): before = lax.ppermute(last, axis, up)  2.39 us
    gather x1, local copies, waits for them, and re-layouts, shift_block(): lax.dynamic_slice_in_dim(segment, SMAX + amount, strip_cols + 2 * tap_rea...  2.01 us
  transfers between devices with their start and end apart: 5, of which 0 were waited for; matrix products, arithmetic and copies ran while one was open for 40% of the time, Pallas kernels for 0%

commit v1 on v0

--- a/solution.py
+++ b/solution.py
@@ -9,6 +9,13 @@
 ROUNDS = 3
 MINI = 8
 ITERS = 3
+
+
+def exchange_blocks(x, name, split, join):
+    peers = lax.axis_size(name)
+    parts = jnp.stack(jnp.split(x, peers, axis=split), axis=0)
+    parts = lax.all_to_all(parts, name, split_axis=0, concat_axis=0)
+    return jnp.concatenate(parts, axis=join)
 
 
 def swapped(value, axis, bit):
@@ -190,9 +197,7 @@
         round_fields = jnp.stack([ifg_re, ifg_im]).reshape(2, date_count, block_pixels)
         ifg_fields.append(round_fields)
     outgoing_all = jnp.take(jnp.concatenate(ifg_fields + [bright_fields], axis=0), inverse, axis=1)
-    linked = link_block(
-        lax.all_to_all(outgoing_all, "date", split_axis=1, concat_axis=1, tiled=True)
-    )
+    linked = link_block(exchange_blocks(outgoing_all, "date", 1, 1))
     return linked.reshape(2, date_count, 2 * block_pixels)
 
 

time: 62.7 us -> 62.8 us (level)
  no operation moved by 1% of the time
where the time goes in v1:
time: 62.8 us; the launch traced here: 62.5 us
  local copies, waits for them, and re-layouts  24.4 us (39%)
  other arithmetic  12.2 us (19%)
  starting transfers between devices  10.4 us (17%)
  blocking collectives  9.29 us (15%)
  between operations  4.98 us (8%)
  matrix products  1.25 us (2%)
    all_to_all x1, blocking collectives, exchange_blocks(): parts = lax.all_to_all(parts, name, split_axis=0, concat_axis=0)  9.29 us
    ppermute x3, starting transfers between devices, swapped(): return lax.ppermute(value, axis, pairs)  6.67 us
    sub x3, local copies, waits for them, and re-layouts, shards(): ifg_im = look_mean(first_im * second_re - first_re * second_im)  6.25 us
    add x3, local copies, waits for them, and re-layouts, shards(): ifg_re = look_mean(first_re * second_re + first_im * second_im)  6.25 us
    add x1, local copies, waits for them, and re-layouts, shards(): brightness = look_mean(centre[0] * centre[0] + centre[1] * centre[1])  5.48 us
    reduce_sum x7, other arithmetic, look_mean(): return jnp.sum(folded, axis=(-3, -1)) * 0.25  4.88 us
    ppermute x1, starting transfers between devices, padded_2(): before = lax.ppermute(last, axis, up)  2.39 us
    gather x1, local copies, waits for them, and re-layouts, shift_block(): lax.dynamic_slice_in_dim(segment, SMAX + amount, strip_cols + 2 * tap_rea...  2.01 us
  transfers between devices with their start and end apart: 5, of which 0 were waited for; matrix products, arithmetic and copies ran while one was open for 40% of the time, Pallas kernels for 0%

profile of v1, /device:TPU:0, one launch (start us, length us, event | category | flops | bytes accessed | tf_op | source)
XLA Modules:
  0.0 62.5 jit_solution(18054526010144742305)
XLA Ops:
  0.0 0.9 %fusion.65 = (f32[2,32,24]{2,1,0:T(8,128)S(1)}, f32[2,32,24]{2,1,0:T(8,128)S(1)}) fusion(f32[2,32,512]{2,1,0:T(8,128)} %bitcast.447), kind=kLoop, calls=%fused_computation.215 | loop fusion | bytes 24576 | tf_op jit(solution)/shard_map/slice | solution.py:32
  0.9 2.4 %collective-permute-start = (f32[2,32,24]{2,1,0:T(8,128)S(1)}, f32[2,32,24]{2,1,0:T(8,128)S(1)}, u32[]{:S(2)}, u32[]{:S(2)}) collective-permute-start(f32[2,32,24]{2,1,0:T(8,128)S(1)} %get-tuple-element.47), channel_id=1, source_target_pairs={{0,1},{2,3},{4,5},{6,7},{8,9},{10,11},{12,13},{14,15},{16,17},{18,... | collective-permute-start | bytes 18440 | tf_op jit(solution)/shard_map/ppermute | solution.py:34
  3.3 1.3 %collective-permute-start.1 = (f32[2,32,24]{2,1,0:T(8,128)S(1)}, f32[2,32,24]{2,1,0:T(8,128)S(1)}, u32[]{:S(2)}, u32[]{:S(2)}) collective-permute-start(f32[2,32,24]{2,1,0:T(8,128)S(1)} %get-tuple-element.48), channel_id=1, source_target_pairs={{1,0},{3,2},{5,4},{7,6},{9,8},{11,10},{13,12},{15,14},{17,16},{19,... | collective-permute-start | bytes 18440 | tf_op jit(solution)/shard_map/ppermute | solution.py:35
  4.6 0.7 %compare_select_fusion.2 = s32[8]{0:T(128)S(1)} fusion(s32[8]{0:T(128)} %param.9), kind=kLoop, calls=%fused_computation.179 | loop fusion | flops 24 | bytes 64 | tf_op jit(solution)/shard_map/select_n | solution.py:173
  5.3 0.6 scatter_custom_fusion
  5.9 1.3 %fusion.45 = (f32[]{:T(128)}, f32[]{:T(128)}, f32[]{:T(128)}, f32[]{:T(128)}) fusion(f32[8]{0:T(128)} %param.7, s32[]{:T(128)S(6)} %xor.11, s32[]{:T(128)S(6)} %axis_index.15, s32[]{:T(128)S(6)} %xor.9, s32[]{:T(128)S(6)} %xor.10), kind=kLoop, calls=%fused_computation.191 | loop fusion | flops 92 | bytes 64 | tf_op jit(solution)/shard_map/reduce_sum | solution.py:179
  11.2 0.7 %or_bitcast_fusion = s32[2]{0:T(128)S(1)} fusion(s32[1,2]{1,0:T(1,128)} %param.6), kind=kLoop, calls=%fused_computation.193 | loop fusion | flops 18 | bytes 16 | tf_op jit(solution)/shard_map/vmap()/gather | solution.py:161
  11.9 0.7 %cosine_multiply_fusion.2 = (f32[17]{0:T(128)S(1)}, f32[17]{0:T(128)S(1)}, f32[17]{0:T(128)S(1)}, f32[17]{0:T(128)S(1)}, f32[17]{0:T(128)S(1)}, /*index=5*/f32[17]{0:T(128)S(1)}) fusion(f32[17]{0:T(128)} %param.8, f32[]{:T(128)S(6)} %mul.430, f32[]{:T(128)S(6)} %mul.445, f32[]{:T(128)S(6)} %mul.460), kind=kLoop, calls=%fused_computation.199 | loop fusion | flops 170 | bytes 488 | tf_op jit(solution)/shard_map/mul | solution.py:104
  12.6 1.0 %select_reduce_fusion = (f32[144,128]{1,0:T(8,128)S(1)}, f32[144,128]{1,0:T(8,128)S(1)}, f32[144,128]{1,0:T(8,128)S(1)}, f32[144,128]{1,0:T(8,128)S(1)}, f32[144,128]{1,0:T(8,128)S(1)}, /*index=5*/f32[144,128]{1,0:T(8,128)S(1)}) fusion(f32[17]{0:T(128)S(1)} %get-tuple-element.68, s32[144,128]{1,0:T(8,128)S(1)} %iota_subtract_fusion, ...), kind=kLoop, calls=%fused_computation.3 | loop fusion | flops 3962880 | bytes 516504 | tf_op jit(solution)/shard_map/reduce_sum | solution.py:112
  14.0 0.8 %copy.101 = f32[2,2,16,560]{2,0,1,3:T(2,128)S(1)} copy(f32[2,2,16,560]{3,2,1,0:T(8,128)S(1)} %pad_maximum_fusion.1) | data formatting | bytes 286720 | tf_op jit(solution)/shard_map/concatenate | solution.py:36
  14.8 2.0 %gather_fusion.1 = f32[2,2,16,528]{2,1,3,0:T(2,128)S(1)} fusion(f32[2,2,16,560]{2,1,0,3:T(2,128)S(1)} %bitcast.438, s32[2]{0:T(128)S(1)} %or_bitcast_fusion), kind=kCustom, calls=%fused_computation.1 | custom fusion | bytes 270368 | tf_op jit(solution)/shard_map/vmap()/gather | solution.py:161
  16.8 0.5 copy.102
  18.1 0.4 fusion
  18.8 3.5 %collective-permute-start.4 = (f32[2,16,512]{2,0,1:T(2,128)S(1)}, f32[2,16,512]{2,0,1:T(2,128)S(1)}, u32[]{:S(2)}, u32[]{:S(2)}) collective-permute-start(f32[2,16,512]{2,0,1:T(2,128)S(1)} %get-tuple-element.36), channel_id=1, source_target_pairs={{0,8},{2,10},{4,12},{6,14},{8,0},{10,2},{12,4},{14,6},{1,9},{3,11}... | collective-permute-start | bytes 196616 | tf_op jit(solution)/shard_map/ppermute | solution.py:24
  22.2 0.4 fusion.2
  22.9 1.6 %collective-permute-start.3 = (f32[2,16,512]{2,0,1:T(2,128)S(1)}, f32[2,16,512]{2,0,1:T(2,128)S(1)}, u32[]{:S(2)}, u32[]{:S(2)}) collective-permute-start(f32[2,16,512]{2,0,1:T(2,128)S(1)} %get-tuple-element.40), channel_id=1, source_target_pairs={{0,4},{2,6},{4,0},{6,2},{8,12},{10,14},{12,8},{14,10},{1,5},{3,7},... | collective-permute-start | bytes 196616 | tf_op jit(solution)/shard_map/ppermute | solution.py:24
  24.6 0.4 fusion.4
  25.2 1.6 %collective-permute-start.2 = (f32[2,16,512]{2,0,1:T(2,128)S(1)}, f32[2,16,512]{2,0,1:T(2,128)S(1)}, u32[]{:S(2)}, u32[]{:S(2)}) collective-permute-start(f32[2,16,512]{2,0,1:T(2,128)S(1)} %get-tuple-element.44), channel_id=1, source_target_pairs={{0,2},{2,0},{4,6},{6,4},{8,10},{10,8},{12,14},{14,12},{1,3},{3,1},... | collective-permute-start | bytes 196616 | tf_op jit(solution)/shard_map/ppermute | solution.py:24
  26.8 5.5 %add.228 = f32[16,2,256,2]{3,2,1,0:T(8,128)} reshape(f32[1,32,512]{2,1,0:T(8,128)S(1)} %fusion.12) | data formatting | bytes 131072 | tf_op jit(solution)/shard_map/add | solution.py:166
  32.3 2.8 %reduce_sum.196 = f32[16,256]{1,0:T(8,128)S(1)} reduce(f32[16,2,256,2]{3,2,1,0:T(8,128)} %add.228, f32[]{:T(128)} %constant.95.clone.1), dimensions={1,3}, to_apply=%region_17.18 | reduce | flops 12288 | bytes 81924 | tf_op jit(solution)/shard_map/reduce_sum | solution.py:43
  35.4 2.1 %add.226 = f32[8,2,256,2]{3,2,1,0:T(8,128)S(1)} reshape(f32[16,512]{1,0:T(8,128)S(1)} %get-tuple-element.6) | data formatting | bytes 65536 | tf_op jit(solution)/shard_map/add | solution.py:195
  37.5 0.3 reduce_sum.194
  37.8 2.1 %sub.173 = f32[8,2,256,2]{3,2,1,0:T(8,128)S(1)} reshape(f32[16,512]{1,0:T(8,128)S(1)} %get-tuple-element.5) | data formatting | bytes 65536 | tf_op jit(solution)/shard_map/sub | solution.py:196
  39.9 0.3 reduce_sum.195
  40.6 2.1 %add.221 = f32[8,2,256,2]{3,2,1,0:T(8,128)S(1)} reshape(f32[16,512]{1,0:T(8,128)S(1)} %get-tuple-element.8) | data formatting | bytes 65536 | tf_op jit(solution)/shard_map/add | solution.py:195
  42.7 0.3 reduce_sum.189
  43.0 2.1 %sub.168 = f32[8,2,256,2]{3,2,1,0:T(8,128)S(1)} reshape(f32[16,512]{1,0:T(8,128)S(1)} %get-tuple-element.7) | data formatting | bytes 65536 | tf_op jit(solution)/shard_map/sub | solution.py:196
  45.8 2.1 %add.216 = f32[8,2,256,2]{3,2,1,0:T(8,128)S(1)} reshape(f32[16,512]{1,0:T(8,128)S(1)} %get-tuple-element.10) | data formatting | bytes 65536 | tf_op jit(solution)/shard_map/add | solution.py:195
  48.3 2.1 %sub.163 = f32[8,2,256,2]{3,2,1,0:T(8,128)S(1)} reshape(f32[16,512]{1,0:T(8,128)S(1)} %get-tuple-element.9) | data formatting | bytes 65536 | tf_op jit(solution)/shard_map/sub | solution.py:196
  50.9 0.6 gather_fusion
  51.6 9.3 %all_to_all.5 = f32[8,8,1,256]{3,1,2,0:T(8,128)S(1)} all-to-all(f32[8,8,1,256]{3,1,2,0:T(8,128)S(1)} %constant_dynamic-update-slice_fusion), channel_id=1, replica_groups=mesh['groups'=2,'date'=8,'strip'=2] {'date'}, dimensions={0} | all-to-all | bytes 131072 | tf_op jit(solution)/shard_map/all_to_all | solution.py:17
  61.9 0.6 pad_maximum_fusion.2
  (115 shorter events, 4.4 us)
Async XLA Ops:
  0.0 13.9 %copy-start = (f32[2,1,32,512]{3,2,1,0:T(8,128)S(1)}, f32[2,1,32,512]{3,2,1,0:T(8,128)}, u32[]{:S(2)}) copy-start(f32[2,1,32,512]{3,2,1,0:T(8,128)} %param.5) | copy-start | bytes 393220
  0.9 13.0 %collective-permute-start = (f32[2,32,24]{2,1,0:T(8,128)S(1)}, f32[2,32,24]{2,1,0:T(8,128)S(1)}, u32[]{:S(2)}, u32[]{:S(2)}) collective-permute-start(f32[2,32,24]{2,1,0:T(8,128)S(1)} %get-tuple-element.47), channel_id=1, source_target_pairs={{0,1},{2,3},{4,5},{6,7},{8,9},{10,11},{12,13},{14,15},{16,17},{18,... | collective-permute-start | bytes 18440 | tf_op jit(solution)/shard_map/ppermute | solution.py:34
  3.3 10.6 %collective-permute-start.1 = (f32[2,32,24]{2,1,0:T(8,128)S(1)}, f32[2,32,24]{2,1,0:T(8,128)S(1)}, u32[]{:S(2)}, u32[]{:S(2)}) collective-permute-start(f32[2,32,24]{2,1,0:T(8,128)S(1)} %get-tuple-element.48), channel_id=1, source_target_pairs={{1,0},{3,2},{5,4},{7,6},{9,8},{11,10},{13,12},{15,14},{17,16},{19,... | collective-permute-start | bytes 18440 | tf_op jit(solution)/shard_map/ppermute | solution.py:35
  18.8 16.4 %collective-permute-start.4 = (f32[2,16,512]{2,0,1:T(2,128)S(1)}, f32[2,16,512]{2,0,1:T(2,128)S(1)}, u32[]{:S(2)}, u32[]{:S(2)}) collective-permute-start(f32[2,16,512]{2,0,1:T(2,128)S(1)} %get-tuple-element.36), channel_id=1, source_target_pairs={{0,8},{2,10},{4,12},{6,14},{8,0},{10,2},{12,4},{14,6},{1,9},{3,11}... | collective-permute-start | bytes 196616 | tf_op jit(solution)/shard_map/ppermute | solution.py:24
  22.9 17.4 %collective-permute-start.3 = (f32[2,16,512]{2,0,1:T(2,128)S(1)}, f32[2,16,512]{2,0,1:T(2,128)S(1)}, u32[]{:S(2)}, u32[]{:S(2)}) collective-permute-start(f32[2,16,512]{2,0,1:T(2,128)S(1)} %get-tuple-element.40), channel_id=1, source_target_pairs={{0,4},{2,6},{4,0},{6,2},{8,12},{10,14},{12,8},{14,10},{1,5},{3,7},... | collective-permute-start | bytes 196616 | tf_op jit(solution)/shard_map/ppermute | solution.py:24
  25.2 20.3 %collective-permute-start.2 = (f32[2,16,512]{2,0,1:T(2,128)S(1)}, f32[2,16,512]{2,0,1:T(2,128)S(1)}, u32[]{:S(2)}, u32[]{:S(2)}) collective-permute-start(f32[2,16,512]{2,0,1:T(2,128)S(1)} %get-tuple-element.44), channel_id=1, source_target_pairs={{0,2},{2,0},{4,6},{6,4},{8,10},{10,8},{12,14},{14,12},{1,3},{3,1},... | collective-permute-start | bytes 196616 | tf_op jit(solution)/shard_map/ppermute | solution.py:24
